TPU v7x, 32 devices: a whole 2x2x4 slice. The times are simulated.
32 devices in a mesh: dp: 4 (over z), mp: 8 (over y, x, core).
Axes of the slice: x: 2, y: 2, z: 4, core: 2. Of those that a mesh axis runs over, the one named last changes fastest.
Arguments:
- block_input: bfloat16 [8192, 2048], P(('dp', 'mp')), may hold values from -6 to 6
- out_cotangent: bfloat16 [8192, 2048], P(('dp', 'mp')), may hold values from -6 to 6
- objective: int32 [16], P('dp'), may hold values from 0 to 1, as said below
- prefix_len: int32 [16], P('dp'), may hold values from 64 to 511
- target_mask: int32 [8192], P(('dp', 'mp')), may hold values from 0 to 1, as said below
- qkv_weight: float32 [2048, 3, 2048], P('dp', None, 'mp'), may hold values from -0.125 to 0.125
- out_weight: float32 [2048, 2048], P('mp', 'dp'), may hold values from -3 to 3
- gateup_weight: float32 [2048, 2, 5472], P('dp', None, 'mp'), may hold values from -0.125 to 0.125
- down_weight: float32 [5472, 2048], P('mp', 'dp'), may hold values from -0.625 to 0.625
- norm_params: float32 [4, 2048], replicated, as said below
- qkv_first: float32 [2048, 3, 2048], P('dp', None, 'mp'), may hold values from -0.125 to 0.125
- out_first: float32 [2048, 2048], P('mp', 'dp'), may hold values from -0.005859375 to 0.005859375
- gateup_first: float32 [2048, 2, 5472], P('dp', None, 'mp'), may hold values from -0.09375 to 0.09375
- down_first: float32 [5472, 2048], P('mp', 'dp'), may hold values from -0.013671875 to 0.013671875
- norm_first: float32 [4, 2048], replicated, may hold values from -0.21875 to 0.21875
- qkv_second: float32 [2048, 3, 2048], P('dp', None, 'mp'), may hold values from 3.0517578e-05 to 0.00048828125
- out_second: float32 [2048, 2048], P('mp', 'dp'), may hold values from 7.080078e-08 to 1.1230469e-06
- gateup_second: float32 [2048, 2, 5472], P('dp', None, 'mp'), may hold values from 1.953125e-05 to 0.0003125
- down_second: float32 [5472, 2048], P('mp', 'dp'), may hold values from 4.3945312e-07 to 7.080078e-06
- norm_second: float32 [4, 2048], replicated, may hold values from 0.00012207031 to 0.001953125
Outputs:
- block_output: bfloat16 [8192, 2048], P(('dp', 'mp'))
- input_grad: float32 [8192, 2048], P(('dp', 'mp'))
- qkv_new: float32 [2048, 3, 2048], P('dp', None, 'mp')
- qkv_first_new: float32 [2048, 3, 2048], P('dp', None, 'mp')
- qkv_second_new: float32 [2048, 3, 2048], P('dp', None, 'mp')
- out_new: float32 [2048, 2048], P('mp', 'dp')
- out_first_new: float32 [2048, 2048], P('mp', 'dp')
- out_second_new: float32 [2048, 2048], P('mp', 'dp')
- gateup_new: float32 [2048, 2, 5472], P('dp', None, 'mp')
- gateup_first_new: float32 [2048, 2, 5472], P('dp', None, 'mp')
- gateup_second_new: float32 [2048, 2, 5472], P('dp', None, 'mp')
- down_new: float32 [5472, 2048], P('mp', 'dp')
- down_first_new: float32 [5472, 2048], P('mp', 'dp')
- down_second_new: float32 [5472, 2048], P('mp', 'dp')
- norm_new: float32 [4, 2048], replicated
- norm_first_new: float32 [4, 2048], replicated
- norm_second_new: float32 [4, 2048], replicated
Inputs may be any that keep to these rules, and one draw needn't show every extreme that they name: `objective`: at least one sequence of each kind. `target_mask`: the last residue of every sequence is a target. `norm_params`: rows 0 and 2 are the gains of the first and second norm, rows 1 and 3 their biases.
All inputs are finite; a program needn't handle non-finite values.
Results may differ from a plain program's by a relative error of at most 0.024.
Values may be sent and summed in bfloat16 or wider, within the bound.
No kernel may reach another device: no remote copies, remote signals or barrier semaphores. Data moves between devices by JAX's collectives and lax.ppermute only.
A program may use at most 256 MiB of HBM per device.

v0:
```python
import jax
import jax.numpy as jnp
from jax import lax
from jax.sharding import PartitionSpec as P

D = 2048
HD = 128
FF = 5461
FF_PAD = 5472
STEP = 5
deep_alpha = 48.0**0.5
norm_eps = 1e-05
masked_score = -1e30
rope_base = 10000.0
beta_one = 0.5
beta_two = 0.5
adam_eps = 1e-08
decay_rate = 0.1


def rope_tables(seq_len, head_dim):
    position = jnp.arange(seq_len, dtype=jnp.float32)
    freqs = rope_base ** (-jnp.arange(0, head_dim, 2, dtype=jnp.float32) / head_dim)
    angles = position[:, None] * freqs[None, :]
    return (jnp.cos(angles), jnp.sin(angles))


def rotate(values, cosine, sine_table):
    half_dim = values.shape[-1] // 2
    first_half = values[..., :half_dim]
    second_half = values[..., half_dim:]
    cos_b = cosine[:, None, :]
    sin_b = sine_table[:, None, :]
    return jnp.concatenate(
        [first_half * cos_b - second_half * sin_b, second_half * cos_b + first_half * sin_b], -1
    )


def norm_forward(hidden, norm_gain, norm_bias):
    row_mean = jnp.mean(hidden, -1, keepdims=True)
    centred = hidden - row_mean
    variance = jnp.mean(centred * centred, -1, keepdims=True)
    inv_std = lax.rsqrt(variance + norm_eps)
    normed = centred * inv_std
    return (normed * norm_gain + norm_bias, normed, inv_std)


def norm_backward(grad_rows, normed, inv_std, norm_gain):
    grad_normed = grad_rows * norm_gain
    mean_grad = jnp.mean(grad_normed, -1, keepdims=True)
    mean_proj = jnp.mean(grad_normed * normed, -1, keepdims=True)
    grad_in = inv_std * (grad_normed - mean_grad - normed * mean_proj)
    return (grad_in, jnp.sum(grad_rows * normed, 0), jnp.sum(grad_rows, 0))


def adamw(weight, gradient, first_moment, second, step_rate):
    first_new = beta_one * first_moment + (1.0 - beta_one) * gradient
    second_new = beta_two * second + (1.0 - beta_two) * gradient * gradient
    first_hat = first_new / (1.0 - beta_one**STEP)
    second_hat = second_new / (1.0 - beta_two**STEP)
    weight_new = weight - step_rate * (
        first_hat / (jnp.sqrt(second_hat) + adam_eps) + decay_rate * weight
    )
    return (weight_new, first_new, second_new)


def local(
    block_input,
    out_cotangent,
    objective,
    prefix_len,
    target_mask,
    qkv_weight,
    out_weight,
    gateup_weight,
    down_weight,
    norm_params,
    qkv_first,
    out_first,
    gateup_first,
    down_first,
    norm_first,
    qkv_second,
    out_second,
    gateup_second,
    down_second,
    norm_second,
):
    mp_count = lax.axis_size("mp")
    mp_index = lax.axis_index("mp")
    own_rows = block_input.shape[0]
    seq_count = objective.shape[0]
    group_rows = own_rows * mp_count
    seq_len = group_rows // seq_count
    local_dim = qkv_weight.shape[2]
    local_heads = local_dim // HD
    local_units = gateup_weight.shape[2]
    score_scale = HD ** (-0.5)
    row_start = mp_index * own_rows
    qkv_full, out_full, gateup_full, down_full = (
        lax.all_gather(qkv_weight.astype(jnp.bfloat16), "dp", axis=0, tiled=True),
        lax.all_gather(out_weight.astype(jnp.bfloat16), "dp", axis=1, tiled=True),
        lax.all_gather(gateup_weight.astype(jnp.bfloat16), "dp", axis=0, tiled=True),
        lax.all_gather(down_weight.astype(jnp.bfloat16), "dp", axis=1, tiled=True),
    )
    input_all = lax.all_gather(block_input, "mp", axis=0, tiled=True)
    projected = jnp.einsum("td,dce->tce", input_all, qkv_full, preferred_element_type=jnp.float32)
    shaped = projected.reshape(seq_count, seq_len, 3, local_heads, HD)
    cosine, sine_table = rope_tables(seq_len, HD)
    query_rows = rotate(shaped[:, :, 0], cosine, sine_table).astype(jnp.bfloat16)
    key_rows = rotate(shaped[:, :, 1], cosine, sine_table).astype(jnp.bfloat16)
    value_rows = shaped[:, :, 2].astype(jnp.bfloat16)
    row_index = jnp.arange(seq_len)[:, None]
    col_index = jnp.arange(seq_len)[None, :]
    visible = (
        (objective[:, None, None] > 0)
        | (col_index[None] < prefix_len[:, None, None])
        | (col_index <= row_index)[None]
    )
    scores = (
        jnp.einsum("sihe,sjhe->shij", query_rows, key_rows, preferred_element_type=jnp.float32)
        * score_scale
    )
    scores = jnp.where(visible[:, None], scores, masked_score)
    row_max = jnp.max(scores, -1, keepdims=True)
    exp_scores = jnp.exp(scores - row_max)
    row_total = jnp.sum(exp_scores, -1, keepdims=True)
    soft_weights = exp_scores / row_total
    log_total = row_max + jnp.log(row_total)
    attended = jnp.einsum(
        "shij,sjhe->sihe",
        soft_weights.astype(jnp.bfloat16),
        value_rows,
        preferred_element_type=jnp.float32,
    )
    attended_low = attended.reshape(group_rows, local_dim).astype(jnp.bfloat16)
    attn_part = jnp.dot(attended_low, out_full, preferred_element_type=jnp.float32)
    attn_total = lax.psum(attn_part, "mp")
    hidden_all = deep_alpha * input_all.astype(jnp.float32) + attn_total
    middle_all, _, _ = norm_forward(hidden_all, norm_params[0], norm_params[1])
    middle_low = middle_all.astype(jnp.bfloat16)
    hidden_one = lax.dynamic_slice_in_dim(hidden_all, row_start, own_rows, 0)
    middle = lax.dynamic_slice_in_dim(middle_all, row_start, own_rows, 0)
    live_units = (mp_index * local_units + jnp.arange(local_units) < FF).astype(jnp.float32)
    gate_up = jnp.einsum("td,dcf->tcf", middle_low, gateup_full, preferred_element_type=jnp.float32)
    hidden_low = (jax.nn.gelu(gate_up[:, 0]) * gate_up[:, 1] * live_units).astype(jnp.bfloat16)
    ffn_part = jnp.dot(hidden_low, down_full, preferred_element_type=jnp.float32)
    ffn_total = lax.psum(ffn_part.astype(jnp.bfloat16), "mp").astype(jnp.float32)
    ffn_own = lax.dynamic_slice_in_dim(ffn_total, row_start, own_rows, 0)
    hidden_two = deep_alpha * middle + ffn_own
    output_rows, normed_two, inv_two = norm_forward(hidden_two, norm_params[2], norm_params[3])
    mask_f32 = target_mask.astype(jnp.float32)
    grad_rows = out_cotangent.astype(jnp.float32) * mask_f32[:, None]
    grad_two, gain_two, bias_two = norm_backward(grad_rows, normed_two, inv_two, norm_params[2])
    ffn_back = lax.all_gather(grad_two.astype(jnp.bfloat16), "mp", axis=0, tiled=True)
    gate_again = jnp.einsum(
        "td,dcf->tcf", middle_low, gateup_full, preferred_element_type=jnp.float32
    )
    gate_act, gelu_pull = jax.vjp(jax.nn.gelu, gate_again[:, 0])
    up_part = gate_again[:, 1]
    hidden_again = (gate_act * up_part * live_units).astype(jnp.bfloat16)
    grad_hidden = (
        jnp.einsum("td,fd->tf", ffn_back, down_full, preferred_element_type=jnp.float32)
        * live_units
    )
    down_grad = jnp.einsum("tf,td->fd", hidden_again, ffn_back, preferred_element_type=jnp.float32)
    grad_gate = gelu_pull(grad_hidden * up_part)[0]
    grad_up = grad_hidden * gate_act
    grad_gateup = jnp.stack([grad_gate, grad_up], 1).astype(jnp.bfloat16)
    middle_part = jnp.einsum(
        "tcf,dcf->td", grad_gateup, gateup_full, preferred_element_type=jnp.float32
    )
    gateup_grad = jnp.einsum(
        "td,tcf->dcf", middle_low, grad_gateup, preferred_element_type=jnp.float32
    )
    grad_middle = (
        lax.psum_scatter(
            middle_part.astype(jnp.bfloat16), "mp", scatter_dimension=0, tiled=True
        ).astype(jnp.float32)
        + deep_alpha * grad_two
    )
    _, normed_one, inv_one = norm_forward(hidden_one, norm_params[0], norm_params[1])
    grad_one, gain_one, bias_one = norm_backward(grad_middle, normed_one, inv_one, norm_params[0])
    attn_back = lax.all_gather(grad_one.astype(jnp.bfloat16), "mp", axis=0, tiled=True)
    grad_attended = jnp.einsum(
        "td,ed->te", attn_back, out_full, preferred_element_type=jnp.float32
    ).astype(jnp.bfloat16)
    grad_attended = grad_attended.reshape(seq_count, seq_len, local_heads, HD)
    out_grad = jnp.einsum("te,td->ed", attended_low, attn_back, preferred_element_type=jnp.float32)
    scores_again = (
        jnp.einsum("sihe,sjhe->shij", query_rows, key_rows, preferred_element_type=jnp.float32)
        * score_scale
    )
    scores_again = jnp.where(visible[:, None], scores_again, masked_score)
    soft_again = jnp.exp(scores_again - log_total)
    grad_soft = jnp.einsum(
        "sihe,sjhe->shij", grad_attended, value_rows, preferred_element_type=jnp.float32
    )
    value_grad = jnp.einsum(
        "shij,sihe->sjhe",
        soft_again.astype(jnp.bfloat16),
        grad_attended,
        preferred_element_type=jnp.float32,
    )
    row_dot = jnp.sum(soft_again * grad_soft, -1, keepdims=True)
    grad_scores = (soft_again * (grad_soft - row_dot)).astype(jnp.bfloat16)
    query_grad = (
        jnp.einsum("shij,sjhe->sihe", grad_scores, key_rows, preferred_element_type=jnp.float32)
        * score_scale
    )
    key_grad = (
        jnp.einsum("shij,sihe->sjhe", grad_scores, query_rows, preferred_element_type=jnp.float32)
        * score_scale
    )
    query_lin = rotate(query_grad, cosine, -sine_table)
    key_lin = rotate(key_grad, cosine, -sine_table)
    grad_proj = (
        jnp.stack([query_lin, key_lin, value_grad], 2)
        .astype(jnp.bfloat16)
        .reshape(group_rows, 3, local_dim)
    )
    input_part = jnp.einsum("tce,dce->td", grad_proj, qkv_full, preferred_element_type=jnp.float32)
    qkv_grad = jnp.einsum("td,tce->dce", input_all, grad_proj, preferred_element_type=jnp.float32)
    input_raw = (
        lax.psum_scatter(
            input_part.astype(jnp.bfloat16), "mp", scatter_dimension=0, tiled=True
        ).astype(jnp.float32)
        + deep_alpha * grad_one
    )
    qkv_grad, out_grad, gateup_grad, down_grad = (
        lax.psum_scatter(
            qkv_grad.astype(jnp.bfloat16), "dp", scatter_dimension=0, tiled=True
        ).astype(jnp.float32),
        lax.psum_scatter(
            out_grad.astype(jnp.bfloat16), "dp", scatter_dimension=1, tiled=True
        ).astype(jnp.float32),
        lax.psum_scatter(
            gateup_grad.astype(jnp.bfloat16), "dp", scatter_dimension=0, tiled=True
        ).astype(jnp.float32),
        lax.psum_scatter(
            down_grad.astype(jnp.bfloat16), "dp", scatter_dimension=1, tiled=True
        ).astype(jnp.float32),
    )
    norm_grad = jnp.stack([gain_one, bias_one, gain_two, bias_two], 0)
    norm_grad, target_count = lax.psum((norm_grad, jnp.sum(mask_f32)), ("dp", "mp"))
    rate_list = (D ** (-0.5), 0.5, D ** (-0.5), (FF_PAD // 64) ** (-0.5), 0.4)
    qkv_res = adamw(qkv_weight, qkv_grad / target_count, qkv_first, qkv_second, rate_list[0])
    out_res = adamw(out_weight, out_grad / target_count, out_first, out_second, rate_list[1])
    gateup_res = adamw(
        gateup_weight, gateup_grad / target_count, gateup_first, gateup_second, rate_list[2]
    )
    down_res = adamw(down_weight, down_grad / target_count, down_first, down_second, rate_list[3])
    norm_res = adamw(norm_params, norm_grad / target_count, norm_first, norm_second, rate_list[4])
    return (
        output_rows.astype(jnp.bfloat16),
        input_raw / target_count,
        qkv_res[0],
        qkv_res[1],
        qkv_res[2],
        out_res[0],
        out_res[1],
        out_res[2],
        gateup_res[0],
        gateup_res[1],
        gateup_res[2],
        down_res[0],
        down_res[1],
        down_res[2],
        norm_res[0],
        norm_res[1],
        norm_res[2],
    )


def solution(mesh):
    return jax.shard_map(
        local,
        mesh=mesh,
        in_specs=(
            P(("dp", "mp"), None),
            P(("dp", "mp"), None),
            P("dp"),
            P("dp"),
            P(("dp", "mp")),
            P("dp", None, "mp"),
            P("mp", "dp"),
            P("dp", None, "mp"),
            P("mp", "dp"),
            P(),
            P("dp", None, "mp"),
            P("mp", "dp"),
            P("dp", None, "mp"),
            P("mp", "dp"),
            P(),
            P("dp", None, "mp"),
            P("mp", "dp"),
            P("dp", None, "mp"),
            P("mp", "dp"),
            P(),
        ),
        out_specs=(
            P(("dp", "mp"), None),
            P(("dp", "mp"), None),
            P("dp", None, "mp"),
            P("dp", None, "mp"),
            P("dp", None, "mp"),
            P("mp", "dp"),
            P("mp", "dp"),
            P("mp", "dp"),
            P("dp", None, "mp"),
            P("dp", None, "mp"),
            P("dp", None, "mp"),
            P("mp", "dp"),
            P("mp", "dp"),
            P("mp", "dp"),
            P(),
            P(),
            P(),
        ),
        check_vma=False,
    )
```

profile of v0, /device:TPU:0, one launch (start us, length us, event | category | flops | bytes accessed | tf_op | source)
XLA Modules:
  0.0 1279.1 jit_solution(2433256142239264889)
XLA Ops:
  14.7 61.7 %all-gather.10.cloned.1.call-done = bf16[2048,3,256]{2,0,1:T(8,128)(2,1)} async-done(((bf16[512,3,256]{2,0,1:T(8,128)(2,1)}), bf16[2048,3,256]{2,0,1:T(8,128)(2,1)}) %all-gather.10.cloned.1.call-update) | async-done | bytes 3145744 | tf_op jit(solution)/shard_map/all_gather | solution.py:101
  76.4 54.8 %all-gather.8.cloned.1.call-done = bf16[2048,2048]{1,0:T(8,128)(2,1)} async-done(((bf16[256,2048]{1,0:T(8,128)(2,1)}), bf16[2048,2048]{1,0:T(8,128)(2,1)}) %all-gather.8.cloned.1.call-update) | async-done | bytes 8388624 | tf_op jit(solution)/shard_map/all_gather | solution.py:106
  131.2 11.6 fusion.6
  142.8 8.3 reshape.239
  173.4 11.4 copy.105
  184.8 9.7 fusion.51
  200.8 211.6 %all-reduce.4.cloned.1.call-done = f32[2048,2048]{1,0:T(8,128)} async-done(((f32[2048,2048]{1,0:T(8,128)}), f32[2048,2048]{1,0:T(8,128)}) %all-reduce.4.cloned.1.call-update) | async-done | bytes 16777232 | tf_op jit(solution)/shard_map/psum | solution.py:138
  412.5 16.0 %fusion.81 = (f32[2048]{0:T(1024)S(1)}, f32[2048,2048]{1,0:T(8,128)}) fusion(f32[2048,2048]{1,0:T(8,128)} %all-reduce.4.cloned.1.call-done, bf16[2048,2048]{1,0:T(8,128)(2,1)} %all-gather.8.cloned.1.call-done), kind=kLoop, calls=%fused_computation.166 | loop fusion | flops 16775168 | bytes 41951232 | tf_op jit(solution)/shard_map/reduce_sum | solution.py:40
  428.5 7.7 multiply_reduce_fusion
  436.2 12.2 multiply_add_fusion
  448.5 69.6 %all-gather.14.cloned.1.call-done = bf16[2048,2,684]{0,1,2:T(2,128)(2,1)} async-done(((bf16[512,2,684]{0,1,2:T(2,128)(2,1)}), bf16[2048,2,684]{0,1,2:T(2,128)(2,1)}) %all-gather.14.cloned.1.call-update) | async-done | bytes 5603344 | tf_op jit(solution)/shard_map/all_gather | solution.py:103
  518.1 22.3 %fusion.2 = f32[2048,2,684]{0,2,1:T(8,128)} fusion(bf16[2048,2,684]{0,1,2:T(2,128)(2,1)} %all-gather.14.cloned.1.call-done, f32[2048,2048]{1,0:T(8,128)} %multiply_add_fusion), kind=kOutput, calls=%fused_computation.7 | convolution fusion | flops 11479810048 | bytes 33587200 | tf_op jit(solution)/shard_map/td,dcf->tcf/dot_general | solution.py:145
  545.8 30.5 %all-gather.16.cloned.1.call-done = bf16[684,2048]{1,0:T(8,128)(2,1)} async-done(((bf16[684,512]{1,0:T(8,128)(2,1)}), bf16[684,2048]{1,0:T(8,128)(2,1)}) %all-gather.16.cloned.1.call-update) | async-done | bytes 2801680 | tf_op jit(solution)/shard_map/all_gather | solution.py:104
  576.3 11.2 convolution_convert_fusion
  588.2 124.4 %all-reduce.6.cloned.1.call-done = bf16[2048,2048]{1,0:T(8,128)(2,1)} async-done(((bf16[2048,2048]{1,0:T(8,128)(2,1)}), bf16[2048,2048]{1,0:T(8,128)(2,1)}) %all-reduce.6.cloned.1.call-update) | async-done | bytes 8388624 | tf_op jit(solution)/shard_map/psum | solution.py:148
  719.2 54.5 %all-gather.18.cloned.1.call-done = bf16[2048,2048]{1,0:T(8,128)(2,1)} async-done(((bf16[256,2048]{1,0:T(8,128)(2,1)}), bf16[2048,2048]{1,0:T(8,128)(2,1)}) %all-gather.18.cloned.1.call-update) | async-done | bytes 8388624 | tf_op jit(solution)/shard_map/all_gather | solution.py:155
  773.7 15.4 %fusion.36 = (bf16[2048,1,684]{0,2,1:T(8,128)(2,1)S(1)}, bf16[2048,1,684]{0,2,1:T(8,128)(2,1)S(1)}) fusion(f32[2048,2,684]{0,2,1:T(8,128)} %fusion.2, f32[684]{0:T(1024)S(1)} %fusion.66, bf16[2048,2048]{1,0:T(8,128)(2,1)} %all-gather.18.cloned.1.call-done, bf16[684,2048]{1,0:T(8,128)(2,1)} %all-gather.16.cloned.1.call-done), kind=kOutput, calls=%fused_computation.56 | convolution fusion | flops 5772828672 | bytes 28002992 | tf_op jit(solution)/shard_map/td,fd->tf/dot_general | solution.py:163
  791.6 17.9 %bitcast_convert_fusion.1 = bf16[2048,2048]{1,0:T(8,128)(2,1)} fusion(bf16[2048,2,684]{0,1,2:T(2,128)(2,1)} %all-gather.14.cloned.1.call-done, bf16[2048,1,684]{0,2,1:T(8,128)(2,1)S(1)} %get-tuple-element.102, bf16[2048,1,684]{0,2,1:T(8,128)(2,1)S(1)} %get-tuple-element.101), kind=kOutput, calls=%fused_computation.1 | convolution fusion | flops 11482611712 | bytes 19595264 | tf_op jit(solution)/shard_map/tcf,dcf->td/dot_general | solution.py:170
  813.5 67.7 %reduce-scatter.7.cloned.1.call-done = bf16[256,2048]{1,0:T(8,128)(2,1)} async-done(((bf16[2048,2048]{1,0:T(8,128)(2,1)}), bf16[256,2048]{1,0:T(8,128)(2,1)}) %reduce-scatter.7.cloned.1.call-update) | async-done | bytes 1048592 | tf_op jit(solution)/shard_map/reduce_scatter | solution.py:177
  888.4 18.6 %fusion.19 = bf16[2048,2,684]{0,2,1:T(8,128)(2,1)} fusion(f32[2048,2048]{1,0:T(8,128)} %multiply_add_fusion, bf16[2048,1,684]{0,2,1:T(8,128)(2,1)} %copy-done.49, bf16[2048,1,684]{0,2,1:T(8,128)(2,1)} %copy-done.48), kind=kOutput, calls=%fused_computation.39 | convolution fusion | flops 11493818368 | bytes 27983872 | tf_op jit(solution)/shard_map/td,tcf->dcf/dot_general | solution.py:173
  908.8 10.6 convolution_convert_fusion.1
  920.2 22.6 %all-gather.20.cloned.1.call-done = bf16[2048,2048]{1,0:T(8,128)(2,1)} async-done(((bf16[256,2048]{1,0:T(8,128)(2,1)}), bf16[2048,2048]{1,0:T(8,128)(2,1)}) %all-gather.20.cloned.1.call-update) | async-done | bytes 8388624 | tf_op jit(solution)/shard_map/all_gather | solution.py:184
  942.7 5.8 convolution_convert_fusion.3
  949.6 6.0 fusion.46
  984.3 6.8 convolution_convert_fusion.2
  993.3 12.0 fusion.31
  1007.1 10.8 bitcast_convert_fusion
  1027.8 41.6 %all-reduce = (f32[]{:T(128)}, f32[4,2048]{1,0:T(4,128)S(1)}) all-reduce(f32[]{:T(128)} %convert_reduce_fusion, f32[4,2048]{1,0:T(4,128)S(1)} %pad_maximum_fusion.11), channel_id=1, replica_groups=mesh['dp'=4,'mp'=8] {'dp','mp'}, use_global_device_ids=true, to_apply=%region_18.19 | all-reduce | flops 8193 | bytes 65544 | tf_op jit(solution)/shard_map/psum | solution.py:245
  1087.2 16.2 %reduce-scatter.17.cloned.1.call-done = bf16[684,512]{1,0:T(8,128)(2,1)} async-done(((bf16[684,2048]{1,0:T(8,128)(2,1)}), bf16[684,512]{1,0:T(8,128)(2,1)}) %reduce-scatter.17.cloned.1.call-update) | async-done | bytes 700432 | tf_op jit(solution)/shard_map/reduce_scatter | solution.py:240
  1108.6 24.2 %reduce-scatter.13.cloned.1.call-done = bf16[256,512]{1,0:T(8,128)(2,1)} async-done(((bf16[256,2048]{1,0:T(8,128)(2,1)}), bf16[256,512]{1,0:T(8,128)(2,1)}) %reduce-scatter.13.cloned.1.call-update) | async-done | bytes 262160 | tf_op jit(solution)/shard_map/reduce_scatter | solution.py:234
  1136.4 57.5 %reduce-scatter.11.cloned.1.call-done = bf16[512,3,256]{0,2,1:T(8,128)(2,1)} async-done(((bf16[2048,3,256]{0,2,1:T(8,128)(2,1)}), bf16[512,3,256]{0,2,1:T(8,128)(2,1)}) %reduce-scatter.11.cloned.1.call-update) | async-done | bytes 786448 | tf_op jit(solution)/shard_map/reduce_scatter | solution.py:231
  1208.9 59.7 %reduce-scatter.9.cloned.1.call-done = bf16[256,2048]{1,0:T(8,128)(2,1)} async-done(((bf16[2048,2048]{1,0:T(8,128)(2,1)}), bf16[256,2048]{1,0:T(8,128)(2,1)}) %reduce-scatter.9.cloned.1.call-update) | async-done | bytes 1048592 | tf_op jit(solution)/shard_map/reduce_scatter | solution.py:225
  (208 shorter events, 153.3 us)
Async XLA Ops:
  7.2 6.0 copy-start.47
  7.2 6.0 copy-start.46
  7.2 69.1 %all-gather.10.cloned.1.call-start = ((), (), s32[]{:S(2)}) async-start(), calls=%async_computation.7 | async-start | bytes 3932160 | tf_op jit(solution)/shard_map/all_gather | solution.py:101
  9.7 121.5 %all-gather.8.cloned.1.call-start = ((), (), s32[]{:S(2)}) async-start(), calls=%async_computation.6 | async-start | bytes 9437184 | tf_op jit(solution)/shard_map/all_gather | solution.py:106
  10.5 174.4 %all-gather.12.cloned.1.call-start = ((), (), s32[]{:S(2)}) async-start(), calls=%async_computation.8 | async-start | bytes 1310720 | tf_op jit(solution)/shard_map/all_gather | solution.py:102
  11.3 401.2 %all-reduce.4.cloned.1.call-start = ((), (), s32[]{:S(2)}) async-start(), calls=%async_computation.9 | async-start | bytes 33554432 | tf_op jit(solution)/shard_map/psum | solution.py:138
  13.2 150.0 %copy-start.26 = (f32[512,64]{1,0:T(8,128)}, f32[512,64]{1,0:T(8,128)S(1)}, u32[]{:S(2)}) copy-start(f32[512,64]{1,0:T(8,128)S(1)} %get-tuple-element.124) | copy-start | bytes 393220
  160.7 8.2 copy-start.14
  184.8 9.7 copy-start.1
  194.5 323.5 %all-gather.14.cloned.1.call-start = ((), (), s32[]{:S(2)}) async-start(), calls=%async_computation.10 | async-start | bytes 7004160 | tf_op jit(solution)/shard_map/all_gather | solution.py:103
  198.4 377.9 %all-gather.16.cloned.1.call-start = ((), (), s32[]{:S(2)}) async-start(), calls=%async_computation.11 | async-start | bytes 3522560 | tf_op jit(solution)/shard_map/all_gather | solution.py:104
  200.7 511.8 %all-reduce.6.cloned.1.call-start = ((), (), s32[]{:S(2)}) async-start(), calls=%async_computation.12 | async-start | bytes 16777216 | tf_op jit(solution)/shard_map/psum | solution.py:148
  545.8 41.6 %copy-start.24 = (bf16[2048,684]{0,1:T(8,128)(2,1)}, bf16[2048,684]{0,1:T(8,128)(2,1)S(1)}, u32[]{:S(2)}) copy-start(bf16[2048,684]{0,1:T(8,128)(2,1)S(1)} %multiply_convert_fusion.2) | copy-start | bytes 8404996
  587.5 186.2 %all-gather.18.cloned.1.call-start = ((), (), s32[]{:S(2)}) async-start(), calls=%async_computation.13 | async-start | bytes 9437184 | tf_op jit(solution)/shard_map/all_gather | solution.py:155
  588.2 127.0 %copy-start.20 = (bf16[256,2048]{1,0:T(8,128)(2,1)S(1)}, bf16[256,2048]{1,0:T(8,128)(2,1)}, u32[]{:S(2)}) copy-start(bf16[256,2048]{1,0:T(8,128)(2,1)} %param.21) | copy-start | bytes 3145732
  719.1 162.0 %reduce-scatter.7.cloned.1.call-start = ((), (), s32[]{:S(2)}) async-start(), calls=%async_computation.14 | async-start | bytes 9437184 | tf_op jit(solution)/shard_map/reduce_scatter | solution.py:177
  809.5 133.2 %all-gather.20.cloned.1.call-start = ((), (), s32[]{:S(2)}) async-start(), calls=%async_computation.15 | async-start | bytes 9437184 | tf_op jit(solution)/shard_map/all_gather | solution.py:184
  888.3 181.1 %reduce-scatter.15.cloned.1.call-start = ((), (), s32[]{:S(2)}) async-start(), calls=%async_computation.19 | async-start | bytes 7045120 | tf_op jit(solution)/shard_map/reduce_scatter | solution.py:237
  907.0 196.4 %reduce-scatter.17.cloned.1.call-start = ((), (), s32[]{:S(2)}) async-start(), calls=%async_computation.20 | async-start | bytes 3522560 | tf_op jit(solution)/shard_map/reduce_scatter | solution.py:240
  919.4 23.3 %copy-start.30 = (bf16[256,2048]{1,0:T(8,128)(2,1)S(1)}, bf16[256,2048]{1,0:T(8,128)(2,1)}, u32[]{:S(2)}) copy-start(bf16[256,2048]{1,0:T(8,128)(2,1)} %all-gather.12.cloned.1.call-done) | copy-start | bytes 3145732
  919.5 213.3 %reduce-scatter.13.cloned.1.call-start = ((), (), s32[]{:S(2)}) async-start(), calls=%async_computation.18 | async-start | bytes 1310720 | tf_op jit(solution)/shard_map/reduce_scatter | solution.py:234
  984.3 6.9 copy-start.22
  991.1 202.7 %reduce-scatter.11.cloned.1.call-start = ((), (), s32[]{:S(2)}) async-start(), calls=%async_computation.17 | async-start | bytes 3932160 | tf_op jit(solution)/shard_map/reduce_scatter | solution.py:231
  1005.3 263.3 %reduce-scatter.9.cloned.1.call-start = ((), (), s32[]{:S(2)}) async-start(), calls=%async_computation.16 | async-start | bytes 9437184 | tf_op jit(solution)/shard_map/reduce_scatter | solution.py:225
  1019.4 5.4 copy-start.40
  1019.4 5.4 copy-start.41
  1021.0 48.5 %copy-start.4 = (f32[512,2,684]{0,1,2:T(2,128)S(1)}, f32[512,2,684]{0,1,2:T(2,128)}, u32[]{:S(2)}) copy-start(f32[512,2,684]{0,1,2:T(2,128)} %param.27) | copy-start | bytes 8404996
  1082.1 21.3 %copy-start.19 = (f32[684,512]{1,0:T(8,128)S(1)}, f32[684,512]{1,0:T(8,128)}, u32[]{:S(2)}) copy-start(f32[684,512]{1,0:T(8,128)} %param.28) | copy-start | bytes 4202500
  1082.1 21.3 %copy-start.29 = (f32[684,512]{1,0:T(8,128)S(1)}, f32[684,512]{1,0:T(8,128)}, u32[]{:S(2)}) copy-start(f32[684,512]{1,0:T(8,128)} %param.33) | copy-start | bytes 4202500
  1108.6 85.3 %copy-start.17 = (f32[512,3,256]{0,2,1:T(8,128)S(1)}, f32[512,3,256]{0,2,1:T(8,128)}, u32[]{:S(2)}) copy-start(f32[512,3,256]{0,2,1:T(8,128)} %copy.125) | copy-start | bytes 4718596
  1108.6 85.3 %copy-start.18 = (f32[512,3,256]{0,2,1:T(8,128)S(1)}, f32[512,3,256]{0,2,1:T(8,128)}, u32[]{:S(2)}) copy-start(f32[512,3,256]{0,2,1:T(8,128)} %copy.121) | copy-start | bytes 4718596
  1202.4 66.2 %copy-start.13 = (f32[256,2048]{1,0:T(8,128)S(1)}, f32[256,2048]{1,0:T(8,128)}, u32[]{:S(2)}) copy-start(f32[256,2048]{1,0:T(8,128)} %get-tuple-element.94) | copy-start | bytes 6291460
  (33 other events, 85.8 us)
Sparse Core Ops, SparseCore 0:
  10.2 66.1 all-gather.9
  78.3 52.8 all-gather.7
  133.3 27.9 all-gather.11
  194.6 217.7 all-reduce.3
  414.4 103.5 all-gather.13
  520.0 56.2 all-gather.15
  587.6 124.8 all-reduce.5
  719.3 54.3 all-gather.17
  809.6 71.4 reduce-scatter.6
  888.5 54.2 all-gather.19
  945.1 100.1 reduce-scatter.14
  1047.4 55.9 reduce-scatter.16
  1105.7 26.9 reduce-scatter.12
  1134.9 58.8 reduce-scatter.10
  1197.2 71.3 reduce-scatter.8
where the time goes:
time: 1290 us; the launch traced here: 1280 us
  waiting for transfers between devices  856 us (66%)
  matrix products  171 us (13%)
  other arithmetic  105 us (8%)
  local copies, waits for them, and re-layouts  89.7 us (7%)
  blocking collectives  41.6 us (3%)
  between operations  15 us (1%)
    psum x1, waiting for transfers between devices, local(): attn_total = lax.psum(attn_part, 'mp')  212 us
    psum x1, waiting for transfers between devices, local(): lax.psum(ffn_part.astype(jnp.bfloat16), 'mp').astype(jnp.float32)  124 us
    all_gather x1, waiting for transfers between devices, local(): lax.all_gather(gateup_weight.astype(jnp.bfloat16), 'dp', axis=0, tiled=True)  69.6 us
    reduce_scatter x1, waiting for transfers between devices, local(): lax.psum_scatter(middle_part.astype(jnp.bfloat16), 'mp', scatter_dimensio...  67.7 us
    all_gather x1, waiting for transfers between devices, local(): lax.all_gather(qkv_weight.astype(jnp.bfloat16), 'dp', axis=0, tiled=True)  61.7 us
    reduce_scatter x1, waiting for transfers between devices, local(): lax.psum_scatter(input_part.astype(jnp.bfloat16), 'mp', scatter_dimension...  59.7 us
    reduce_scatter x1, waiting for transfers between devices, local(): lax.psum_scatter(qkv_grad.astype(jnp.bfloat16), 'dp', scatter_dimension=0...  57.5 us
    all_gather x1, waiting for transfers between devices, local(): input_all = lax.all_gather(block_input, 'mp', axis=0, tiled=True)  54.8 us
  transfers between devices with their start and end apart: 15, of which 13 were waited for; matrix products, arithmetic and copies ran while one was open for 22% of the time, Pallas kernels for 0%

commit v1 on v0

--- a/solution.py
+++ b/solution.py
@@ -16,6 +16,19 @@
 beta_two = 0.5
 adam_eps = 1e-08
 decay_rate = 0.1
+
+
+def ring_gather(value, axis, dim):
+    ways = lax.axis_size(axis)
+    up = [(d, (d + 1) % ways) for d in range(ways)]
+    down = [(d, (d - 1) % ways) for d in range(ways)]
+    earlier, later = ([value], [value])
+    for _ in range(ways // 2):
+        earlier.append(lax.ppermute(earlier[-1], axis, up))
+    for _ in range((ways - 1) // 2):
+        later.append(lax.ppermute(later[-1], axis, down))
+    line = jnp.concatenate([*earlier[::-1], *later[1:]], axis=dim)
+    return jnp.roll(line, (lax.axis_index(axis) - ways // 2) * value.shape[dim], axis=dim)
 
 
 def rope_tables(seq_len, head_dim):
@@ -152,7 +165,7 @@
     mask_f32 = target_mask.astype(jnp.float32)
     grad_rows = out_cotangent.astype(jnp.float32) * mask_f32[:, None]
     grad_two, gain_two, bias_two = norm_backward(grad_rows, normed_two, inv_two, norm_params[2])
-    ffn_back = lax.all_gather(grad_two.astype(jnp.bfloat16), "mp", axis=0, tiled=True)
+    ffn_back = ring_gather(grad_two.astype(jnp.bfloat16), "mp", 0)
     gate_again = jnp.einsum(
         "td,dcf->tcf", middle_low, gateup_full, preferred_element_type=jnp.float32
     )

time: 1290 us -> 1350 us (1.047)
  waiting for transfers between devices: 856 us -> 887 us
  local copies, waits for them, and re-layouts: 89.7 us -> 115 us
    ppermute x0 -> x7, waiting for transfers between devices: none -> 85.4 us  [the longest x4 85.4 us: ring_gather(): earlier.append(lax.ppermute(earlier[-1], axis, up))]
    all_gather x1 -> x0, waiting for transfers between devices: 54.5 us -> none  [local(): lax.all_gather(grad_two.astype(jnp.bfloat16), 'mp', axis=0, tiled=True)]
    unnamed x112 -> x141, local copies, waits for them, and re-layouts: 47.2 us -> 71.2 us
  transfers between devices with their start and end apart: 15 -> 21, of which waited for: 13 -> 16; matrix products, arithmetic and copies ran while one was open for 22% -> 22% of each run, Pallas kernels for 0% -> 0%
where the time goes in v1:
time: 1350 us; the launch traced here: 1340 us
  waiting for transfers between devices  887 us (66%)
  matrix products  173 us (13%)
  local copies, waits for them, and re-layouts  115 us (9%)
  other arithmetic  104 us (8%)
  blocking collectives  41.4 us (3%)
  between operations  15.1 us (1%)
    psum x1, waiting for transfers between devices, local(): attn_total = lax.psum(attn_part, 'mp')  212 us
    psum x1, waiting for transfers between devices, local(): lax.psum(ffn_part.astype(jnp.bfloat16), 'mp').astype(jnp.float32)  124 us
    ppermute x4, waiting for transfers between devices, ring_gather(): earlier.append(lax.ppermute(earlier[-1], axis, up))  85.4 us
    unnamed x141, local copies, waits for them, and re-layouts  71.2 us
    all_gather x1, waiting for transfers between devices, local(): lax.all_gather(gateup_weight.astype(jnp.bfloat16), 'dp', axis=0, tiled=True)  69.6 us
    reduce_scatter x1, waiting for transfers between devices, local(): lax.psum_scatter(middle_part.astype(jnp.bfloat16), 'mp', scatter_dimensio...  67.5 us
    all_gather x1, waiting for transfers between devices, local(): lax.all_gather(qkv_weight.astype(jnp.bfloat16), 'dp', axis=0, tiled=True)  61.7 us
    reduce_scatter x1, waiting for transfers between devices, local(): lax.psum_scatter(input_part.astype(jnp.bfloat16), 'mp', scatter_dimension...  59.7 us
  transfers between devices with their start and end apart: 21, of which 16 were waited for; matrix products, arithmetic and copies ran while one was open for 22% of the time, Pallas kernels for 0%

profile of v1, /device:TPU:0, one launch (start us, length us, event | category | flops | bytes accessed | tf_op | source)
XLA Modules:
  0.0 1344.0 jit_solution(15949026294555650534)
XLA Ops:
  14.7 61.7 %all-gather.9.cloned.1.call-done = bf16[2048,3,256]{2,0,1:T(8,128)(2,1)} async-done(((bf16[512,3,256]{2,0,1:T(8,128)(2,1)}), bf16[2048,3,256]{2,0,1:T(8,128)(2,1)}) %all-gather.9.cloned.1.call-update) | async-done | bytes 3145744 | tf_op jit(solution)/shard_map/all_gather | solution.py:114
  76.4 54.8 %all-gather.7.cloned.1.call-done = bf16[2048,2048]{1,0:T(8,128)(2,1)} async-done(((bf16[256,2048]{1,0:T(8,128)(2,1)}), bf16[2048,2048]{1,0:T(8,128)(2,1)}) %all-gather.7.cloned.1.call-update) | async-done | bytes 8388624 | tf_op jit(solution)/shard_map/all_gather | solution.py:119
  131.2 11.6 fusion.6
  142.8 8.3 reshape.239
  173.4 11.4 copy.105
  184.8 9.7 fusion.58
  200.9 211.6 %all-reduce.4.cloned.1.call-done = f32[2048,2048]{1,0:T(8,128)} async-done(((f32[2048,2048]{1,0:T(8,128)}), f32[2048,2048]{1,0:T(8,128)}) %all-reduce.4.cloned.1.call-update) | async-done | bytes 16777232 | tf_op jit(solution)/shard_map/psum | solution.py:151
  412.5 16.0 %fusion.90 = (f32[2048]{0:T(1024)S(1)}, f32[2048,2048]{1,0:T(8,128)}) fusion(f32[2048,2048]{1,0:T(8,128)} %all-reduce.4.cloned.1.call-done, bf16[2048,2048]{1,0:T(8,128)(2,1)} %all-gather.7.cloned.1.call-done), kind=kLoop, calls=%fused_computation.188 | loop fusion | flops 16775168 | bytes 41951232 | tf_op jit(solution)/shard_map/reduce_sum | solution.py:53
  428.5 7.7 multiply_reduce_fusion
  436.2 12.2 multiply_add_fusion
  448.5 69.6 %all-gather.13.cloned.1.call-done = bf16[2048,2,684]{0,1,2:T(2,128)(2,1)} async-done(((bf16[512,2,684]{0,1,2:T(2,128)(2,1)}), bf16[2048,2,684]{0,1,2:T(2,128)(2,1)}) %all-gather.13.cloned.1.call-update) | async-done | bytes 5603344 | tf_op jit(solution)/shard_map/all_gather | solution.py:116
  518.1 22.2 %fusion.2 = f32[2048,2,684]{0,2,1:T(8,128)} fusion(bf16[2048,2,684]{0,1,2:T(2,128)(2,1)} %all-gather.13.cloned.1.call-done, f32[2048,2048]{1,0:T(8,128)} %multiply_add_fusion), kind=kOutput, calls=%fused_computation.7 | convolution fusion | flops 11479810048 | bytes 33587200 | tf_op jit(solution)/shard_map/td,dcf->tcf/dot_general | solution.py:158
  545.9 30.5 %all-gather.15.cloned.1.call-done = bf16[684,2048]{1,0:T(8,128)(2,1)} async-done(((bf16[684,512]{1,0:T(8,128)(2,1)}), bf16[684,2048]{1,0:T(8,128)(2,1)}) %all-gather.15.cloned.1.call-update) | async-done | bytes 2801680 | tf_op jit(solution)/shard_map/all_gather | solution.py:117
  576.3 11.0 convolution_convert_fusion
  588.0 124.4 %all-reduce.6.cloned.1.call-done = bf16[2048,2048]{1,0:T(8,128)(2,1)} async-done(((bf16[2048,2048]{1,0:T(8,128)(2,1)}), bf16[2048,2048]{1,0:T(8,128)(2,1)}) %all-reduce.6.cloned.1.call-update) | async-done | bytes 8388624 | tf_op jit(solution)/shard_map/psum | solution.py:161
  718.6 15.1 %collective-permute-done = bf16[256,2048]{1,0:T(8,128)(2,1)S(1)} collective-permute-done((bf16[256,2048]{1,0:T(8,128)(2,1)S(1)}, bf16[256,2048]{1,0:T(8,128)(2,1)S(1)}, u32[]{:S(2)}, u32[]{:S(2)}) %collective-permute-start) | collective-permute-done | bytes 1048608 | tf_op jit(solution)/shard_map/ppermute | solution.py:27
  736.4 23.6 %collective-permute-done.1 = bf16[256,2048]{1,0:T(8,128)(2,1)S(1)} collective-permute-done((bf16[256,2048]{1,0:T(8,128)(2,1)S(1)}, bf16[256,2048]{1,0:T(8,128)(2,1)S(1)}, u32[]{:S(2)}, u32[]{:S(2)}) %collective-permute-start.1) | collective-permute-done | bytes 1048608 | tf_op jit(solution)/shard_map/ppermute | solution.py:27
  762.6 23.5 %collective-permute-done.2 = bf16[256,2048]{1,0:T(8,128)(2,1)} collective-permute-done((bf16[256,2048]{1,0:T(8,128)(2,1)S(1)}, bf16[256,2048]{1,0:T(8,128)(2,1)}, u32[]{:S(2)}, u32[]{:S(2)}) %collective-permute-start.2) | collective-permute-done | bytes 1048608 | tf_op jit(solution)/shard_map/ppermute | solution.py:27
  788.8 23.1 %collective-permute-done.3 = bf16[256,2048]{1,0:T(8,128)(2,1)} collective-permute-done((bf16[256,2048]{1,0:T(8,128)(2,1)}, bf16[256,2048]{1,0:T(8,128)(2,1)}, u32[]{:S(2)}, u32[]{:S(2)}) %collective-permute-start.3) | collective-permute-done | bytes 1048608 | tf_op jit(solution)/shard_map/ppermute | solution.py:27
  839.4 14.3 %fusion.43 = (bf16[2048,1,684]{0,2,1:T(8,128)(2,1)}, bf16[2048,1,684]{0,2,1:T(8,128)(2,1)}) fusion(f32[2048,2,684]{0,2,1:T(8,128)S(1)} %bitcast.110, f32[684]{0:T(1024)S(1)} %fusion.73, bf16[684,2048]{1,0:T(8,128)(2,1)S(1)} %copy-done.52, bf16[4096,2048]{1,0:T(8,128)(2,1)} %constant_dynamic-update-slice_fusion, s32[]{:T(128)S(6)} %select_n.26), kind=kOutput, calls=%fused_computation.60 | convolution fusion | flops 5772828672 | bytes 28002996 | tf_op jit(solution)/shard_map/td,fd->tf/dot_general | solution.py:176
  853.8 20.9 %bitcast_convert_fusion.1 = bf16[2048,2048]{1,0:T(8,128)(2,1)} fusion(bf16[2048,2,684]{0,1,2:T(2,128)(2,1)} %all-gather.13.cloned.1.call-done, bf16[2048,1,684]{0,2,1:T(8,128)(2,1)} %get-tuple-element.102, bf16[2048,1,684]{0,2,1:T(8,128)(2,1)} %get-tuple-element.101), kind=kOutput, calls=%fused_computation.1 | convolution fusion | flops 11482611712 | bytes 19595264 | tf_op jit(solution)/shard_map/tcf,dcf->td/dot_general | solution.py:183
  878.7 67.5 %reduce-scatter.7.cloned.1.call-done = bf16[256,2048]{1,0:T(8,128)(2,1)} async-done(((bf16[2048,2048]{1,0:T(8,128)(2,1)}), bf16[256,2048]{1,0:T(8,128)(2,1)}) %reduce-scatter.7.cloned.1.call-update) | async-done | bytes 1048592 | tf_op jit(solution)/shard_map/reduce_scatter | solution.py:190
  953.5 18.7 %fusion.23 = bf16[2048,2,684]{0,2,1:T(8,128)(2,1)} fusion(f32[2048,2048]{1,0:T(8,128)} %multiply_add_fusion, bf16[2048,1,684]{0,2,1:T(8,128)(2,1)} %get-tuple-element.102, bf16[2048,1,684]{0,2,1:T(8,128)(2,1)} %get-tuple-element.101), kind=kOutput, calls=%fused_computation.43 | convolution fusion | flops 11493818368 | bytes 27983872 | tf_op jit(solution)/shard_map/td,tcf->dcf/dot_general | solution.py:186
  973.9 10.6 fusion.35
  985.3 22.5 %all-gather.17.cloned.1.call-done = bf16[2048,2048]{1,0:T(8,128)(2,1)} async-done(((bf16[256,2048]{1,0:T(8,128)(2,1)}), bf16[2048,2048]{1,0:T(8,128)(2,1)}) %all-gather.17.cloned.1.call-update) | async-done | bytes 8388624 | tf_op jit(solution)/shard_map/all_gather | solution.py:197
  1058.4 12.0 fusion.38
  1072.3 10.8 bitcast_convert_fusion
  1093.0 41.4 %all-reduce = (f32[]{:T(128)}, f32[4,2048]{1,0:T(4,128)S(1)}) all-reduce(f32[]{:T(128)} %convert_reduce_fusion, f32[4,2048]{1,0:T(4,128)S(1)} %pad_maximum_fusion.11), channel_id=1, replica_groups=mesh['dp'=4,'mp'=8] {'dp','mp'}, use_global_device_ids=true, to_apply=%region_18.19 | all-reduce | flops 8193 | bytes 65544 | tf_op jit(solution)/shard_map/psum | solution.py:258
  1152.1 16.4 %reduce-scatter.17.cloned.1.call-done = bf16[684,512]{1,0:T(8,128)(2,1)} async-done(((bf16[684,2048]{1,0:T(8,128)(2,1)}), bf16[684,512]{1,0:T(8,128)(2,1)}) %reduce-scatter.17.cloned.1.call-update) | async-done | bytes 700432 | tf_op jit(solution)/shard_map/reduce_scatter | solution.py:253
  1173.5 24.1 %reduce-scatter.13.cloned.1.call-done = bf16[256,512]{1,0:T(8,128)(2,1)} async-done(((bf16[256,2048]{1,0:T(8,128)(2,1)}), bf16[256,512]{1,0:T(8,128)(2,1)}) %reduce-scatter.13.cloned.1.call-update) | async-done | bytes 262160 | tf_op jit(solution)/shard_map/reduce_scatter | solution.py:247
  1201.1 57.7 %reduce-scatter.11.cloned.1.call-done = bf16[512,3,256]{0,2,1:T(8,128)(2,1)} async-done(((bf16[2048,3,256]{0,2,1:T(8,128)(2,1)}), bf16[512,3,256]{0,2,1:T(8,128)(2,1)}) %reduce-scatter.11.cloned.1.call-update) | async-done | bytes 786448 | tf_op jit(solution)/shard_map/reduce_scatter | solution.py:244
  1273.9 59.7 %reduce-scatter.9.cloned.1.call-done = bf16[256,2048]{1,0:T(8,128)(2,1)} async-done(((bf16[2048,2048]{1,0:T(8,128)(2,1)}), bf16[256,2048]{1,0:T(8,128)(2,1)}) %reduce-scatter.9.cloned.1.call-update) | async-done | bytes 1048592 | tf_op jit(solution)/shard_map/reduce_scatter | solution.py:238
  (250 shorter events, 204.1 us)
Async XLA Ops:
  7.2 69.1 %all-gather.9.cloned.1.call-start = ((), (), s32[]{:S(2)}) async-start(), calls=%async_computation.7 | async-start | bytes 3932160 | tf_op jit(solution)/shard_map/all_gather | solution.py:114
  9.7 121.5 %all-gather.7.cloned.1.call-start = ((), (), s32[]{:S(2)}) async-start(), calls=%async_computation.6 | async-start | bytes 9437184 | tf_op jit(solution)/shard_map/all_gather | solution.py:119
  10.5 174.4 %all-gather.11.cloned.1.call-start = ((), (), s32[]{:S(2)}) async-start(), calls=%async_computation.8 | async-start | bytes 1310720 | tf_op jit(solution)/shard_map/all_gather | solution.py:115
  11.3 401.2 %all-reduce.4.cloned.1.call-start = ((), (), s32[]{:S(2)}) async-start(), calls=%async_computation.9 | async-start | bytes 33554432 | tf_op jit(solution)/shard_map/psum | solution.py:151
  13.2 150.0 %copy-start.31 = (f32[512,64]{1,0:T(8,128)}, f32[512,64]{1,0:T(8,128)S(1)}, u32[]{:S(2)}) copy-start(f32[512,64]{1,0:T(8,128)S(1)} %get-tuple-element.124) | copy-start | bytes 393220
  194.6 323.5 %all-gather.13.cloned.1.call-start = ((), (), s32[]{:S(2)}) async-start(), calls=%async_computation.10 | async-start | bytes 7004160 | tf_op jit(solution)/shard_map/all_gather | solution.py:116
  198.4 377.9 %all-gather.15.cloned.1.call-start = ((), (), s32[]{:S(2)}) async-start(), calls=%async_computation.11 | async-start | bytes 3522560 | tf_op jit(solution)/shard_map/all_gather | solution.py:117
  200.8 511.6 %all-reduce.6.cloned.1.call-start = ((), (), s32[]{:S(2)}) async-start(), calls=%async_computation.12 | async-start | bytes 16777216 | tf_op jit(solution)/shard_map/psum | solution.py:161
  545.8 41.4 %copy-start.29 = (bf16[2048,684]{0,1:T(8,128)(2,1)}, bf16[2048,684]{0,1:T(8,128)(2,1)S(1)}, u32[]{:S(2)}) copy-start(bf16[2048,684]{0,1:T(8,128)(2,1)S(1)} %multiply_convert_fusion.2) | copy-start | bytes 8404996
  587.3 358.9 %reduce-scatter.7.cloned.1.call-start = ((), (), s32[]{:S(2)}) async-start(), calls=%async_computation.13 | async-start | bytes 9437184 | tf_op jit(solution)/shard_map/reduce_scatter | solution.py:190
  588.0 127.0 %copy-start.20 = (bf16[256,2048]{1,0:T(8,128)(2,1)S(1)}, bf16[256,2048]{1,0:T(8,128)(2,1)}, u32[]{:S(2)}) copy-start(bf16[256,2048]{1,0:T(8,128)(2,1)} %param.21) | copy-start | bytes 3145732
  718.6 15.1 %collective-permute-start = (bf16[256,2048]{1,0:T(8,128)(2,1)S(1)}, bf16[256,2048]{1,0:T(8,128)(2,1)S(1)}, u32[]{:S(2)}, u32[]{:S(2)}) collective-permute-start(bf16[256,2048]{1,0:T(8,128)(2,1)S(1)} %get-tuple-element.95), channel_id=1, source_target_pairs={{0,1},{1,2},{2,3},{3,4},{4,5},{5,6},{6,7},{7,0},{8,9},{9,10},{10,1... | collective-permute-start | bytes 3145736 | tf_op jit(solution)/shard_map/ppermute | solution.py:27
  733.7 26.3 %copy-start.22 = (bf16[256,2048]{1,0:T(8,128)(2,1)}, bf16[256,2048]{1,0:T(8,128)(2,1)S(1)}, u32[]{:S(2)}) copy-start(bf16[256,2048]{1,0:T(8,128)(2,1)S(1)} %collective-permute-done) | copy-start | bytes 3145732
  733.7 26.3 %collective-permute-start.1 = (bf16[256,2048]{1,0:T(8,128)(2,1)S(1)}, bf16[256,2048]{1,0:T(8,128)(2,1)S(1)}, u32[]{:S(2)}, u32[]{:S(2)}) collective-permute-start(bf16[256,2048]{1,0:T(8,128)(2,1)S(1)} %collective-permute-done), channel_id=1, source_target_pairs={{0,1},{1,2},{2,3},{3,4},{4,5},{5,6},{6,7},{7,0},{8,9},{9,10},{10,1... | collective-permute-start | bytes 3145736 | tf_op jit(solution)/shard_map/ppermute | solution.py:27
  733.7 26.3 %collective-permute-start.4 = (bf16[256,2048]{1,0:T(8,128)(2,1)S(1)}, bf16[256,2048]{1,0:T(8,128)(2,1)}, u32[]{:S(2)}, u32[]{:S(2)}) collective-permute-start(bf16[256,2048]{1,0:T(8,128)(2,1)S(1)} %get-tuple-element.95), channel_id=1, source_target_pairs={{0,7},{1,0},{2,1},{3,2},{4,3},{5,4},{6,5},{7,6},{8,15},{9,8},{10,9... | collective-permute-start | bytes 3145736 | tf_op jit(solution)/shard_map/ppermute | solution.py:29
  760.0 26.2 %collective-permute-start.2 = (bf16[256,2048]{1,0:T(8,128)(2,1)S(1)}, bf16[256,2048]{1,0:T(8,128)(2,1)}, u32[]{:S(2)}, u32[]{:S(2)}) collective-permute-start(bf16[256,2048]{1,0:T(8,128)(2,1)S(1)} %collective-permute-done.1), channel_id=1, source_target_pairs={{0,1},{1,2},{2,3},{3,4},{4,5},{5,6},{6,7},{7,0},{8,9},{9,10},{10,1... | collective-permute-start | bytes 3145736 | tf_op jit(solution)/shard_map/ppermute | solution.py:27
  760.0 26.2 %collective-permute-start.5 = (bf16[256,2048]{1,0:T(8,128)(2,1)}, bf16[256,2048]{1,0:T(8,128)(2,1)}, u32[]{:S(2)}, u32[]{:S(2)}) collective-permute-start(bf16[256,2048]{1,0:T(8,128)(2,1)} %collective-permute-done.4), channel_id=1, source_target_pairs={{0,7},{1,0},{2,1},{3,2},{4,3},{5,4},{6,5},{7,6},{8,15},{9,8},{10,9... | collective-permute-start | bytes 3145736 | tf_op jit(solution)/shard_map/ppermute | solution.py:29
  786.2 25.8 %collective-permute-start.3 = (bf16[256,2048]{1,0:T(8,128)(2,1)}, bf16[256,2048]{1,0:T(8,128)(2,1)}, u32[]{:S(2)}, u32[]{:S(2)}) collective-permute-start(bf16[256,2048]{1,0:T(8,128)(2,1)} %collective-permute-done.2), channel_id=1, source_target_pairs={{0,1},{1,2},{2,3},{3,4},{4,5},{5,6},{6,7},{7,0},{8,9},{9,10},{10,1... | collective-permute-start | bytes 3145736 | tf_op jit(solution)/shard_map/ppermute | solution.py:27
  786.2 30.4 %copy-start.25 = (bf16[256,2048]{1,0:T(8,128)(2,1)S(1)}, bf16[256,2048]{1,0:T(8,128)(2,1)}, u32[]{:S(2)}) copy-start(bf16[256,2048]{1,0:T(8,128)(2,1)} %copy-done.24) | copy-start | bytes 3145732
  786.2 31.4 %copy-start.23 = (bf16[256,2048]{1,0:T(8,128)(2,1)S(1)}, bf16[256,2048]{1,0:T(8,128)(2,1)}, u32[]{:S(2)}) copy-start(bf16[256,2048]{1,0:T(8,128)(2,1)} %copy-done.22) | copy-start | bytes 3145732
  786.2 38.3 %collective-permute-start.6 = (bf16[256,2048]{1,0:T(8,128)(2,1)}, bf16[256,2048]{1,0:T(8,128)(2,1)S(1)}, u32[]{:S(2)}, u32[]{:S(2)}) collective-permute-start(bf16[256,2048]{1,0:T(8,128)(2,1)} %collective-permute-done.5), channel_id=1, source_target_pairs={{0,7},{1,0},{2,1},{3,2},{4,3},{5,4},{6,5},{7,6},{8,15},{9,8},{10,9... | collective-permute-start | bytes 3145736 | tf_op jit(solution)/shard_map/ppermute | solution.py:29
  874.7 133.1 %all-gather.17.cloned.1.call-start = ((), (), s32[]{:S(2)}) async-start(), calls=%async_computation.14 | async-start | bytes 9437184 | tf_op jit(solution)/shard_map/all_gather | solution.py:197
  953.4 181.0 %reduce-scatter.15.cloned.1.call-start = ((), (), s32[]{:S(2)}) async-start(), calls=%async_computation.18 | async-start | bytes 7045120 | tf_op jit(solution)/shard_map/reduce_scatter | solution.py:250
  972.2 196.3 %reduce-scatter.17.cloned.1.call-start = ((), (), s32[]{:S(2)}) async-start(), calls=%async_computation.19 | async-start | bytes 3522560 | tf_op jit(solution)/shard_map/reduce_scatter | solution.py:253
  984.6 23.3 %copy-start.35 = (bf16[256,2048]{1,0:T(8,128)(2,1)S(1)}, bf16[256,2048]{1,0:T(8,128)(2,1)}, u32[]{:S(2)}) copy-start(bf16[256,2048]{1,0:T(8,128)(2,1)} %all-gather.11.cloned.1.call-done) | copy-start | bytes 3145732
  984.6 213.0 %reduce-scatter.13.cloned.1.call-start = ((), (), s32[]{:S(2)}) async-start(), calls=%async_computation.17 | async-start | bytes 1310720 | tf_op jit(solution)/shard_map/reduce_scatter | solution.py:247
  1056.3 202.6 %reduce-scatter.11.cloned.1.call-start = ((), (), s32[]{:S(2)}) async-start(), calls=%async_computation.16 | async-start | bytes 3932160 | tf_op jit(solution)/shard_map/reduce_scatter | solution.py:244
  1070.4 263.2 %reduce-scatter.9.cloned.1.call-start = ((), (), s32[]{:S(2)}) async-start(), calls=%async_computation.15 | async-start | bytes 9437184 | tf_op jit(solution)/shard_map/reduce_scatter | solution.py:238
  1086.1 48.2 %copy-start.4 = (f32[512,2,684]{0,1,2:T(2,128)S(1)}, f32[512,2,684]{0,1,2:T(2,128)}, u32[]{:S(2)}) copy-start(f32[512,2,684]{0,1,2:T(2,128)} %param.27) | copy-start | bytes 8404996
  1173.5 85.3 %copy-start.17 = (f32[512,3,256]{0,2,1:T(8,128)S(1)}, f32[512,3,256]{0,2,1:T(8,128)}, u32[]{:S(2)}) copy-start(f32[512,3,256]{0,2,1:T(8,128)} %copy.125) | copy-start | bytes 4718596
  1173.5 85.3 %copy-start.18 = (f32[512,3,256]{0,2,1:T(8,128)S(1)}, f32[512,3,256]{0,2,1:T(8,128)}, u32[]{:S(2)}) copy-start(f32[512,3,256]{0,2,1:T(8,128)} %copy.121) | copy-start | bytes 4718596
  1267.3 66.3 %copy-start.13 = (f32[256,2048]{1,0:T(8,128)S(1)}, f32[256,2048]{1,0:T(8,128)}, u32[]{:S(2)}) copy-start(f32[256,2048]{1,0:T(8,128)} %get-tuple-element.94) | copy-start | bytes 6291460
  (46 other events, 223.2 us)
Sparse Core Ops, SparseCore 0:
  10.2 66.1 all-gather.8
  78.3 52.8 all-gather.6
  133.3 27.9 all-gather.10
  194.7 217.7 all-reduce.3
  414.5 103.5 all-gather.12
  520.1 56.2 all-gather.14
  587.4 124.8 all-reduce.5
  874.8 71.3 reduce-scatter.6
  953.5 54.2 all-gather.16
  1010.0 100.1 reduce-scatter.14
  1112.5 55.8 reduce-scatter.16
  1170.6 26.9 reduce-scatter.12
  1199.9 58.9 reduce-scatter.10
  1262.2 71.4 reduce-scatter.8
